TPU v7x, 256 devices: a whole 4x4x8 slice. The times are simulated.
256 devices in a mesh: seq: 8 (over y_lo, x), chan: 32 (over z, y_hi, core).
Axes of the slice: x: 4, y: 4 (y_hi: 2, y_lo: 2; y = y_hi * 2 + y_lo), z: 8, core: 2. Of those that a mesh axis runs over, the one named last changes fastest.
Arguments:
- post_gate: bfloat16 [2048, 8192], P('chan', 'seq'), may hold values from -6 to 6
- pre_gate: bfloat16 [2048, 8192], P('chan', 'seq'), may hold values from -6 to 6
- signal: bfloat16 [2048, 8192], P('chan', 'seq'), may hold values from -6 to 6
- cotangent: bfloat16 [2048, 8192], P('chan', 'seq'), may hold values from -6 to 6
- filter_taps: float32 [2048, 8192], P('chan', 'seq'), may hold values from -0.0625 to 0.0625
- skip_gain: float32 [2048], P('chan'), may hold values from -4 to 4
Outputs:
- output: bfloat16 [2048, 8192], P('chan', 'seq')
- d_post: bfloat16 [2048, 8192], P('chan', 'seq')
- d_pre: bfloat16 [2048, 8192], P('chan', 'seq')
- d_signal: bfloat16 [2048, 8192], P('chan', 'seq')
- d_skip: float32 [2048], P('chan')
- d_filter: float32 [2048, 8192], P('chan', 'seq')
All inputs are finite; a program needn't handle non-finite values.
Results may differ from a plain program's by a relative error of at most 0.004.
Values sent between devices are 32-bit elements; how exact they have to be, the bound alone decides.
A program may use at most 64 MiB of HBM per device.

v0:
```python
import functools
import math

import jax
import jax.numpy as jnp
import numpy as np
from jax import lax
from jax.experimental import pallas as pl
from jax.experimental.pallas import tpu as pltpu
from jax.sharding import PartitionSpec as P

LANES = 128
SUB = 8
F32 = jnp.float32
BF16 = jnp.bfloat16


def halves(table):
    high = table.astype(jnp.bfloat16)
    low = (table - high.astype(np.float64)).astype(jnp.bfloat16)
    return high, low


def tables(rows, padded):
    a = np.arange(rows)[:, None]
    b = np.arange(rows)[None, :] + 0.5
    theta = 2.0 * math.pi * a * b / (2 * rows)
    first = np.concatenate([np.cos(theta).T, -np.sin(theta).T], axis=0)
    last = np.concatenate([np.cos(theta), np.sin(theta)], axis=1) * (2.0 / padded)
    r = np.arange(LANES)
    phi = 2.0 * math.pi * (np.arange(rows)[:, None] + 0.5) * r[None, :] / padded
    turn = np.stack([np.cos(phi), -np.sin(phi)]).astype(np.float32)
    psi = 2.0 * math.pi * np.outer(r, r) / LANES
    cos_m, sin_m = np.cos(psi), np.sin(psi)
    mid = np.block([[cos_m, -sin_m], [sin_m, cos_m]])
    f_hi, f_lo = halves(first)
    m_hi, m_lo = halves(mid)
    l_hi, l_lo = halves(last)
    return (
        np.concatenate([f_hi, f_hi, f_lo], axis=1),
        np.concatenate([m_hi, m_hi, m_lo], axis=0),
        np.concatenate([l_hi, l_hi, l_lo], axis=1),
        turn,
    )


def split(value, axis):
    high = value.astype(BF16)
    low = (value - high.astype(F32)).astype(BF16)
    return jnp.concatenate([high, low, high], axis=axis)


def dot(left, right):
    return jnp.dot(left, right, preferred_element_type=F32)


def kernel(
    n, chunks,
    post, pre, sig, cot, taps, skip, first, mid, last, turn,
    o_out, o_post, o_pre, o_sig, o_skip, o_taps,
    sbuf, rbuf, obuf, gbuf, dsum, dgot,
    self_sem, s_in, r_in, s_out, r_out, s_sum, r_sum,
):
    me = lax.axis_index("seq")
    chans, length = taps.shape
    blocks = length // LANES
    own = chans // n
    rows = n * blocks
    per = own // chunks
    step = per * blocks
    scale = 1.0 / math.sqrt(n * length)

    barrier = pltpu.get_barrier_semaphore()
    for k in range(1, n):
        pl.semaphore_signal(barrier, inc=1, device_id={"seq": lax.rem(me + k, n)})

    for pair in range(n // 2):
        for q in range(blocks):
            at = (slice(2 * SUB * pair, 2 * SUB * (pair + 1)), slice(LANES * q, LANES * (q + 1)))
            gated = pre[at].astype(F32) * sig[at].astype(F32)
            slope = cot[at].astype(F32) * post[at].astype(F32)
            tap = taps[at]
            for half in range(2):
                cut = slice(SUB * half, SUB * (half + 1))
                to = (2 * pair + half, pl.ds(q, SUB, stride=blocks), slice(None))
                sbuf[(0,) + to] = tap[cut]
                sbuf[(1,) + to] = gated[cut]
                sbuf[(2,) + to] = slope[cut]

    pl.semaphore_wait(barrier, n - 1)

    def inward(c, k):
        part = pl.ds(pl.multiple_of(c * step, step), step)
        return pltpu.make_async_remote_copy(
            src_ref=sbuf.at[:, lax.rem(me + k, n), part],
            dst_ref=rbuf.at[:, me, part],
            send_sem=s_in.at[c, k], recv_sem=r_in.at[c, k],
            device_id={"seq": lax.rem(me + k, n)},
        )

    def outward(c, k):
        part = pl.ds(pl.multiple_of(c * step, step), step)
        return pltpu.make_async_remote_copy(
            src_ref=obuf.at[:, lax.rem(me + k, n), part],
            dst_ref=gbuf.at[:, me, part],
            send_sem=s_out.at[c, k], recv_sem=r_out.at[c, k],
            device_id={"seq": lax.rem(me + k, n)},
        )

    def summed(k):
        return pltpu.make_async_remote_copy(
            src_ref=dsum, dst_ref=dgot.at[me],
            send_sem=s_sum.at[k], recv_sem=r_sum.at[k],
            device_id={"seq": lax.rem(me + k, n)},
        )

    def mine(which, c):
        part = pl.ds(pl.multiple_of(c * step, step), step)
        src, dst = ((sbuf, rbuf), (obuf, gbuf))[which]
        return pltpu.make_async_copy(src.at[:, me, part], dst.at[:, me, part], self_sem.at[which, c])

    for c in range(chunks):
        for k in range(1, n):
            inward(c, k).start()
        mine(0, c).start()

    def chunk(c, carry):
        for k in range(1, n):
            inward(c, k).wait()
        mine(0, c).wait()
        base = pl.multiple_of(c * step, step)
        grown = []
        for f in range(3):
            xs = []
            for i in range(per):
                xs.append(rbuf[f, :, pl.ds(base + i * blocks, blocks), :].reshape(rows, LANES))
            if f == 1:
                gates = xs
            if f == 2:
                for i in range(per):
                    dsum[pl.ds(c * per + i, 1), :] = jnp.sum(gates[i] * xs[i], axis=0, keepdims=True)
            x = jnp.concatenate(xs, axis=1)
            y = dot(first[...], split(x, 0))
            for i in range(per):
                cut = slice(LANES * i, LANES * (i + 1))
                re, im = y[:rows, cut], y[rows:, cut]
                grown.append(jnp.concatenate([re * turn[0] - im * turn[1], re * turn[1] + im * turn[0]], axis=1))
        spec = dot(split(jnp.concatenate(grown, axis=0), 1), mid[...])
        prods = [[], [], []]
        for i in range(per):
            parts = []
            for f in range(3):
                top = (f * per + i) * rows
                parts.append((spec[top:top + rows, :LANES], spec[top:top + rows, LANES:]))
            (hr, hi), (gr, gi), (dr, di) = parts
            prods[0].append(jnp.concatenate([hr * gr - hi * gi, -(hr * gi + hi * gr)], axis=1))
            prods[1].append(jnp.concatenate([hr * dr + hi * di, hi * dr - hr * di], axis=1))
            prods[2].append(jnp.concatenate([gr * dr + gi * di, gi * dr - gr * di], axis=1))
        back = dot(split(jnp.concatenate(prods[0] + prods[1] + prods[2], axis=0), 1), mid[...])
        for f in range(3):
            cols = []
            for i in range(per):
                top = (f * per + i) * rows
                re, im = back[top:top + rows, :LANES], back[top:top + rows, LANES:]
                cols.append(jnp.concatenate([re * turn[0] - im * turn[1], re * turn[1] + im * turn[0]], axis=0))
            out = dot(last[...], split(jnp.concatenate(cols, axis=1), 0))
            for i in range(per):
                obuf[f, :, pl.ds(base + i * blocks, blocks), :] = out[:, LANES * i:LANES * (i + 1)].reshape(n, blocks, LANES)
        for k in range(1, n):
            outward(c, k).start()
        mine(1, c).start()
        return carry

    lax.fori_loop(0, chunks, chunk, 0)
    for k in range(1, n):
        summed(k).start()

    lane = lax.broadcasted_iota(jnp.int32, (chans, chans), 1)
    row = lax.broadcasted_iota(jnp.int32, (chans, chans), 0)
    gain = jnp.sum(jnp.where(lane == row, jnp.broadcast_to(skip[...], (chans, chans)), 0.0), axis=1, keepdims=True)

    for c in range(chunks):
        for k in range(1, n):
            outward(c, k).wait()
        mine(1, c).wait()
    for k in range(1, n):
        summed(k).wait()
    dgot[me] = dsum[...]

    for pair in range(n // 2):
        down = slice(2 * SUB * pair, 2 * SUB * (pair + 1))
        col = jnp.broadcast_to(gain[down], (2 * SUB, LANES))
        for q in range(blocks):
            at = (down, slice(LANES * q, LANES * (q + 1)))
            got = []
            for f in range(3):
                got.append(jnp.concatenate([gbuf[f, 2 * pair + half, pl.ds(q, SUB, stride=blocks), :] for half in range(2)], axis=0))
            post_f, pre_f = post[at].astype(F32), pre[at].astype(F32)
            sig_f, cot_f = sig[at].astype(F32), cot[at].astype(F32)
            conved = got[0] + col * (pre_f * sig_f)
            o_out[at] = (post_f * conved).astype(BF16)
            o_post[at] = (cot_f * conved).astype(BF16)
            d_gated = got[1] + col * (cot_f * post_f)
            o_pre[at] = (d_gated * sig_f).astype(BF16)
            o_sig[at] = (d_gated * pre_f).astype(BF16)
            o_taps[at] = got[2] * scale
    total = jnp.sum(dgot[...].reshape(chans, LANES), axis=1, keepdims=True) * scale
    o_skip[...] = jnp.sum(jnp.where(lane == row, jnp.broadcast_to(total, (chans, chans)), 0.0), axis=0, keepdims=True)


def solution(mesh):
    n = mesh.shape["seq"]
    chunks = 4

    def shards(post_gate, pre_gate, signal, cotangent, filter_taps, skip_gain):
        chans, length = filter_taps.shape
        blocks = length // LANES
        own = chans // n
        first, mid, last, turn = tables(n * blocks, 2 * n * length)
        vmem = pl.BlockSpec(memory_space=pltpu.VMEM)
        small = jax.ShapeDtypeStruct((chans, length), BF16)
        buf = pltpu.VMEM((3, n, own * blocks, LANES), F32)
        sem = pltpu.SemaphoreType.DMA((chunks, n))
        outs = pl.pallas_call(
            functools.partial(kernel, n, chunks),
            out_shape=(small, small, small, small, jax.ShapeDtypeStruct((1, chans), F32), jax.ShapeDtypeStruct((chans, length), F32)),
            in_specs=[vmem] * 10,
            out_specs=[vmem] * 6,
            scratch_shapes=[
                buf, buf, buf, buf,
                pltpu.VMEM((own, LANES), F32), pltpu.VMEM((n, own, LANES), F32),
                pltpu.SemaphoreType.DMA((2, chunks)), sem, sem, sem, sem,
                pltpu.SemaphoreType.DMA((n,)), pltpu.SemaphoreType.DMA((n,)),
            ],
            compiler_params=pltpu.CompilerParams(collective_id=0, has_side_effects=True, vmem_limit_bytes=48 << 20),
        )(post_gate, pre_gate, signal, cotangent, filter_taps, skip_gain.reshape(1, chans), first, mid, last, turn)
        return outs[0], outs[1], outs[2], outs[3], outs[4].reshape(chans), outs[5]

    return jax.shard_map(
        shards,
        mesh=mesh,
        in_specs=(P("chan", "seq"),) * 5 + (P("chan"),),
        out_specs=(P("chan", "seq"),) * 4 + (P("chan"), P("chan", "seq")),
        check_vma=False,
    )
```

profile of v0, /device:TPU:32, one launch (start us, length us, event | category | flops | bytes accessed | tf_op | source)
XLA Modules:
  0.0 37.7 jit_solution(18103525383708257025)
XLA Ops:
  0.6 0.0 copy-start.9
  0.6 0.6 %copy-done.9 = f32[64]{0:T(128)S(1)} copy-done((f32[64]{0:T(128)S(1)}, f32[64]{0:T(128)}, u32[]{:S(2)}) %copy-start.9) | copy-done | bytes 280
  1.3 0.0 copy-start
  1.3 1.0 %copy-done = bf16[768,256]{1,0:T(8,128)(2,1)S(1)} copy-done((bf16[768,256]{1,0:T(8,128)(2,1)S(1)}, bf16[768,256]{1,0:T(8,128)(2,1)}, u32[]{:S(2)}) %copy-start) | copy-done | bytes 393240
  2.3 0.0 copy-start.1
  2.3 0.9 %copy-done.1 = f32[64,1024]{1,0:T(8,128)S(1)} copy-done((f32[64,1024]{1,0:T(8,128)S(1)}, f32[64,1024]{1,0:T(8,128)}, u32[]{:S(2)}) %copy-start.1) | copy-done | bytes 262168
  3.2 0.0 copy-start.2
  3.2 0.9 %copy-done.2 = bf16[64,1024]{1,0:T(8,128)(2,1)S(1)} copy-done((bf16[64,1024]{1,0:T(8,128)(2,1)S(1)}, bf16[64,1024]{1,0:T(8,128)(2,1)}, u32[]{:S(2)}) %copy-start.2) | copy-done | bytes 131096
  4.1 0.0 copy-start.3
  4.1 0.9 %copy-done.3 = bf16[64,1024]{1,0:T(8,128)(2,1)S(1)} copy-done((bf16[64,1024]{1,0:T(8,128)(2,1)S(1)}, bf16[64,1024]{1,0:T(8,128)(2,1)}, u32[]{:S(2)}) %copy-start.3) | copy-done | bytes 131096
  5.0 0.0 copy-start.4
  5.0 0.9 %copy-done.4 = bf16[64,1024]{1,0:T(8,128)(2,1)S(1)} copy-done((bf16[64,1024]{1,0:T(8,128)(2,1)S(1)}, bf16[64,1024]{1,0:T(8,128)(2,1)}, u32[]{:S(2)}) %copy-start.4) | copy-done | bytes 131096
  6.0 0.0 copy-start.5
  6.0 0.9 %copy-done.5 = bf16[64,1024]{1,0:T(8,128)(2,1)S(1)} copy-done((bf16[64,1024]{1,0:T(8,128)(2,1)S(1)}, bf16[64,1024]{1,0:T(8,128)(2,1)}, u32[]{:S(2)}) %copy-start.5) | copy-done | bytes 131096
  6.9 0.0 copy-start.6
  6.9 0.8 %copy-done.6 = f32[2,64,128]{2,1,0:T(8,128)S(1)} copy-done((f32[2,64,128]{2,1,0:T(8,128)S(1)}, f32[2,64,128]{2,1,0:T(8,128)}, u32[]{:S(2)}) %copy-start.6) | copy-done | bytes 65560
  7.7 0.0 copy-start.7
  7.7 0.8 %copy-done.7 = bf16[128,192]{1,0:T(8,128)(2,1)S(1)} copy-done((bf16[128,192]{1,0:T(8,128)(2,1)S(1)}, bf16[128,192]{1,0:T(8,128)(2,1)}, u32[]{:S(2)}) %copy-start.7) | copy-done | bytes 49176
  8.5 0.0 copy-start.8
  8.5 0.8 %copy-done.8 = bf16[64,384]{1,0:T(8,128)(2,1)S(1)} copy-done((bf16[64,384]{1,0:T(8,128)(2,1)S(1)}, bf16[64,384]{1,0:T(8,128)(2,1)}, u32[]{:S(2)}) %copy-start.8) | copy-done | bytes 49176
  9.3 24.5 %shard_map.145 = (bf16[64,1024]{1,0:T(8,128)(2,1)S(1)}, bf16[64,1024]{1,0:T(8,128)(2,1)S(1)}, bf16[64,1024]{1,0:T(8,128)(2,1)S(1)}, bf16[64,1024]{1,0:T(8,128)(2...) custom-call(bf16[64,1024]{1,0:T(8,128)(2,1)S(1)} %copy-done.2, bf16[64,1024]{1,0:T(8,128)(2,1)S(1)} %copy-done.3, ...), custom_call_target="tpu_custom_call" | custom-call | tf_op jit(solution)/shard_map/pallas_call | solution.py:224
  33.8 0.7 %copy.22 = bf16[64,1024]{1,0:T(8,128)(2,1)} copy(bf16[64,1024]{1,0:T(8,128)(2,1)S(1)} %get-tuple-element.24) | data formatting | bytes 262144
  34.5 0.7 %copy.23 = bf16[64,1024]{1,0:T(8,128)(2,1)} copy(bf16[64,1024]{1,0:T(8,128)(2,1)S(1)} %get-tuple-element.25) | data formatting | bytes 262144
  35.1 0.7 %copy.24 = bf16[64,1024]{1,0:T(8,128)(2,1)} copy(bf16[64,1024]{1,0:T(8,128)(2,1)S(1)} %get-tuple-element.26) | data formatting | bytes 262144
  35.8 0.7 %copy.25 = bf16[64,1024]{1,0:T(8,128)(2,1)} copy(bf16[64,1024]{1,0:T(8,128)(2,1)S(1)} %get-tuple-element.27) | data formatting | bytes 262144
  36.4 0.5 %copy.26 = f32[64]{0:T(128)} copy(f32[64]{0:T(128)S(1)} %bitcast.3) | data formatting | bytes 512
  37.0 0.7 %copy.27 = f32[64,1024]{1,0:T(8,128)} copy(f32[64,1024]{1,0:T(8,128)S(1)} %get-tuple-element.29) | data formatting | bytes 524288
Async XLA Ops:
  0.6 0.7 %copy-start.9 = (f32[64]{0:T(128)S(1)}, f32[64]{0:T(128)}, u32[]{:S(2)}) copy-start(f32[64]{0:T(128)} %param.15) | copy-start | bytes 772
  1.3 1.0 %copy-start = (bf16[768,256]{1,0:T(8,128)(2,1)S(1)}, bf16[768,256]{1,0:T(8,128)(2,1)}, u32[]{:S(2)}) copy-start(bf16[768,256]{1,0:T(8,128)(2,1)} %constant.9.clone.mid) | copy-start | bytes 1179652
  2.3 0.9 %copy-start.1 = (f32[64,1024]{1,0:T(8,128)S(1)}, f32[64,1024]{1,0:T(8,128)}, u32[]{:S(2)}) copy-start(f32[64,1024]{1,0:T(8,128)} %taps.1) | copy-start | bytes 786436
  3.2 0.9 %copy-start.2 = (bf16[64,1024]{1,0:T(8,128)(2,1)S(1)}, bf16[64,1024]{1,0:T(8,128)(2,1)}, u32[]{:S(2)}) copy-start(bf16[64,1024]{1,0:T(8,128)(2,1)} %post.1) | copy-start | bytes 393220
  4.1 0.9 %copy-start.3 = (bf16[64,1024]{1,0:T(8,128)(2,1)S(1)}, bf16[64,1024]{1,0:T(8,128)(2,1)}, u32[]{:S(2)}) copy-start(bf16[64,1024]{1,0:T(8,128)(2,1)} %pre.1) | copy-start | bytes 393220
  5.0 0.9 %copy-start.4 = (bf16[64,1024]{1,0:T(8,128)(2,1)S(1)}, bf16[64,1024]{1,0:T(8,128)(2,1)}, u32[]{:S(2)}) copy-start(bf16[64,1024]{1,0:T(8,128)(2,1)} %sig.1) | copy-start | bytes 393220
  6.0 0.9 %copy-start.5 = (bf16[64,1024]{1,0:T(8,128)(2,1)S(1)}, bf16[64,1024]{1,0:T(8,128)(2,1)}, u32[]{:S(2)}) copy-start(bf16[64,1024]{1,0:T(8,128)(2,1)} %cot.1) | copy-start | bytes 393220
  6.9 0.8 %copy-start.6 = (f32[2,64,128]{2,1,0:T(8,128)S(1)}, f32[2,64,128]{2,1,0:T(8,128)}, u32[]{:S(2)}) copy-start(f32[2,64,128]{2,1,0:T(8,128)} %constant.11.clone.turn) | copy-start | bytes 196612
  7.7 0.8 %copy-start.7 = (bf16[128,192]{1,0:T(8,128)(2,1)S(1)}, bf16[128,192]{1,0:T(8,128)(2,1)}, u32[]{:S(2)}) copy-start(bf16[128,192]{1,0:T(8,128)(2,1)} %constant.8.clone.first) | copy-start | bytes 147460
  8.5 0.8 %copy-start.8 = (bf16[64,384]{1,0:T(8,128)(2,1)S(1)}, bf16[64,384]{1,0:T(8,128)(2,1)}, u32[]{:S(2)}) copy-start(bf16[64,384]{1,0:T(8,128)(2,1)} %constant.10.clone.last) | copy-start | bytes 147460
where the time goes:
time: 38 us; the launch traced here: 37.7 us
  Pallas kernels  24.5 us (64%)
  local copies, waits for them, and re-layouts  12.5 us (33%)
  between operations  0.66 us (2%)
    pallas_call x1, Pallas kernels, shards(): pl.pallas_call(functools.partial(kernel, n, chunks), out_shape=(small, sm...  24.5 us
    unnamed x26, local copies, waits for them, and re-layouts  12.5 us

commit v1 on v0

--- a/solution.py
+++ b/solution.py
@@ -54,12 +54,19 @@
     return jnp.dot(left, right, preferred_element_type=F32)
 
 
-def kernel(
+def fill(pairs, sems):
+    copies = [pltpu.make_async_copy(src, dst, sems.at[i]) for i, (src, dst) in enumerate(pairs)]
+    for copy in copies:
+        copy.start()
+    return copies
+
+
+def exchange(
     n, chunks,
-    post, pre, sig, cot, taps, skip, first, mid, last, turn,
-    o_out, o_post, o_pre, o_sig, o_skip, o_taps,
-    sbuf, rbuf, obuf, gbuf, dsum, dgot,
-    self_sem, s_in, r_in, s_out, r_out, s_sum, r_sum,
+    h_post, h_pre, h_sig, h_cot, h_taps, h_first, h_mid, h_last, h_turn, h_skip,
+    gbuf, dgot, post, pre, sig, cot, skip,
+    taps, first, mid, last, turn, sbuf, rbuf, obuf, dsum,
+    load_sem, self_sem, s_in, r_in, s_out, r_out, s_sum, r_sum,
 ):
     me = lax.axis_index("seq")
     chans, length = taps.shape
@@ -68,11 +75,15 @@
     rows = n * blocks
     per = own // chunks
     step = per * blocks
-    scale = 1.0 / math.sqrt(n * length)
 
     barrier = pltpu.get_barrier_semaphore()
     for k in range(1, n):
         pl.semaphore_signal(barrier, inc=1, device_id={"seq": lax.rem(me + k, n)})
+    loads = fill(
+        [(h_taps, taps), (h_pre, pre), (h_sig, sig), (h_cot, cot), (h_post, post),
+         (h_first, first), (h_mid, mid), (h_turn, turn), (h_last, last), (h_skip, skip)], load_sem)
+    for load in loads[:5]:
+        load.wait()
 
     for pair in range(n // 2):
         for q in range(blocks):
@@ -123,6 +134,9 @@
         for k in range(1, n):
             inward(c, k).start()
         mine(0, c).start()
+
+    for load in loads[5:]:
+        load.wait()
 
     def chunk(c, carry):
         for k in range(1, n):
@@ -175,9 +189,6 @@
     for k in range(1, n):
         summed(k).start()
 
-    lane = lax.broadcasted_iota(jnp.int32, (chans, chans), 1)
-    row = lax.broadcasted_iota(jnp.int32, (chans, chans), 0)
-    gain = jnp.sum(jnp.where(lane == row, jnp.broadcast_to(skip[...], (chans, chans)), 0.0), axis=1, keepdims=True)
 
     for c in range(chunks):
         for k in range(1, n):
@@ -187,6 +198,18 @@
         summed(k).wait()
     dgot[me] = dsum[...]
 
+
+def finish(n, gbuf, dgot, post, pre, sig, cot, skip, h_out, h_post, h_pre, h_sig, h_skip, h_taps,
+           o_out, o_post, o_pre, o_sig, o_skip, o_taps, sems):
+    chans, length = post.shape
+    blocks = length // LANES
+    scale = 1.0 / math.sqrt(n * length)
+    lane = lax.broadcasted_iota(jnp.int32, (chans, chans), 1)
+    row = lax.broadcasted_iota(jnp.int32, (chans, chans), 0)
+    gain = jnp.sum(jnp.where(lane == row, jnp.broadcast_to(skip[...], (chans, chans)), 0.0), axis=1, keepdims=True)
+    total = jnp.sum(dgot[...].reshape(chans, LANES), axis=1, keepdims=True) * scale
+    o_skip[...] = jnp.sum(jnp.where(lane == row, jnp.broadcast_to(total, (chans, chans)), 0.0), axis=0, keepdims=True)
+    stores = fill([(o_skip, h_skip)], sems.at[n // 2])
     for pair in range(n // 2):
         down = slice(2 * SUB * pair, 2 * SUB * (pair + 1))
         col = jnp.broadcast_to(gain[down], (2 * SUB, LANES))
@@ -204,8 +227,10 @@
             o_pre[at] = (d_gated * sig_f).astype(BF16)
             o_sig[at] = (d_gated * pre_f).astype(BF16)
             o_taps[at] = got[2] * scale
-    total = jnp.sum(dgot[...].reshape(chans, LANES), axis=1, keepdims=True) * scale
-    o_skip[...] = jnp.sum(jnp.where(lane == row, jnp.broadcast_to(total, (chans, chans)), 0.0), axis=0, keepdims=True)
+        stores += fill([(src.at[down], dst.at[down]) for src, dst in
+                        ((o_out, h_out), (o_post, h_post), (o_pre, h_pre), (o_sig, h_sig), (o_taps, h_taps))], sems.at[pair])
+    for store in stores:
+        store.wait()
 
 
 def solution(mesh):
@@ -218,22 +243,39 @@
         own = chans // n
         first, mid, last, turn = tables(n * blocks, 2 * n * length)
         vmem = pl.BlockSpec(memory_space=pltpu.VMEM)
-        small = jax.ShapeDtypeStruct((chans, length), BF16)
-        buf = pltpu.VMEM((3, n, own * blocks, LANES), F32)
+        hbm = pl.BlockSpec(memory_space=pltpu.HBM)
+        half = jax.ShapeDtypeStruct((chans, length), BF16)
+        full = jax.ShapeDtypeStruct((chans, length), F32)
+        line = jax.ShapeDtypeStruct((1, chans), F32)
+        fields = (3, n, own * blocks, LANES)
+        buf = pltpu.VMEM(fields, F32)
         sem = pltpu.SemaphoreType.DMA((chunks, n))
-        outs = pl.pallas_call(
-            functools.partial(kernel, n, chunks),
-            out_shape=(small, small, small, small, jax.ShapeDtypeStruct((1, chans), F32), jax.ShapeDtypeStruct((chans, length), F32)),
-            in_specs=[vmem] * 10,
-            out_specs=[vmem] * 6,
+        got = pl.pallas_call(
+            functools.partial(exchange, n, chunks),
+            out_shape=(jax.ShapeDtypeStruct(fields, F32), jax.ShapeDtypeStruct((n, own, LANES), F32), half, half, half, half, line),
+            in_specs=[hbm] * 10,
+            out_specs=[vmem] * 7,
             scratch_shapes=[
-                buf, buf, buf, buf,
-                pltpu.VMEM((own, LANES), F32), pltpu.VMEM((n, own, LANES), F32),
+                pltpu.VMEM((chans, length), F32),
+                pltpu.VMEM(first.shape, BF16), pltpu.VMEM(mid.shape, BF16), pltpu.VMEM(last.shape, BF16), pltpu.VMEM(turn.shape, F32),
+                buf, buf, buf,
+                pltpu.VMEM((own, LANES), F32),
+                pltpu.SemaphoreType.DMA((10,)),
                 pltpu.SemaphoreType.DMA((2, chunks)), sem, sem, sem, sem,
                 pltpu.SemaphoreType.DMA((n,)), pltpu.SemaphoreType.DMA((n,)),
             ],
-            compiler_params=pltpu.CompilerParams(collective_id=0, has_side_effects=True, vmem_limit_bytes=48 << 20),
-        )(post_gate, pre_gate, signal, cotangent, filter_taps, skip_gain.reshape(1, chans), first, mid, last, turn)
+            compiler_params=pltpu.CompilerParams(collective_id=0, has_side_effects=True, vmem_limit_bytes=32 << 20),
+        )(*[pltpu.with_memory_space_constraint(x, pltpu.HBM) for x in (
+            post_gate, pre_gate, signal, cotangent, filter_taps, first, mid, last, turn, skip_gain.reshape(1, chans))])
+        outs = pl.pallas_call(
+            functools.partial(finish, n),
+            out_shape=(half, half, half, half, line, full),
+            in_specs=[vmem] * 7,
+            out_specs=[hbm] * 6,
+            scratch_shapes=[pltpu.VMEM((chans, length), BF16)] * 4 + [
+                pltpu.VMEM((1, chans), F32), pltpu.VMEM((chans, length), F32), pltpu.SemaphoreType.DMA((n // 2 + 1, 5))],
+            compiler_params=pltpu.CompilerParams(vmem_limit_bytes=32 << 20),
+        )(*got)
         return outs[0], outs[1], outs[2], outs[3], outs[4].reshape(chans), outs[5]
 
     return jax.shard_map(

time: 38 us -> 26.8 us (0.71)
  local copies, waits for them, and re-layouts: 12.5 us -> 0 us
  Pallas kernels: 24.5 us -> 26.1 us
    unnamed x26 -> x0, local copies, waits for them, and re-layouts: 12.5 us -> none
    pallas_call x1 -> x2, Pallas kernels: 24.5 us -> 26.1 us  [the longest x1 24.8 us: shards(): pl.pallas_call(functools.partial(exchange, n, chunks), out_shape=(jax.Sha...]
where the time goes in v1:
time: 26.8 us; the launch traced here: 26.7 us
  Pallas kernels  26.1 us (97%)
  between operations  0.64 us (2%)
    pallas_call x1, Pallas kernels, shards(): pl.pallas_call(functools.partial(exchange, n, chunks), out_shape=(jax.Sha...  24.8 us
    pallas_call x1, Pallas kernels, shards(): pl.pallas_call(functools.partial(finish, n), out_shape=(half, half, half,...  1.29 us

profile of v1, /device:TPU:32, one launch (start us, length us, event | category | flops | bytes accessed | tf_op | source)
XLA Modules:
  0.0 26.7 jit_solution(11754446296292342902)
XLA Ops:
  0.6 24.8 %shard_map.145 = (f32[3,8,64,128]{3,2,1,0:T(8,128)S(1)}, f32[8,8,128]{2,1,0:T(8,128)S(1)}, bf16[64,1024]{1,0:T(8,128)(2,1)S(1)}, bf16[64,1024]{1,0:T(8,128)(2,1)...) custom-call(bf16[64,1024]{1,0:T(8,128)(2,1)} %h_post.1, ...), custom_call_target="tpu_custom_call" | custom-call | tf_op jit(solution)/shard_map/pallas_call | solution.py:253
  25.4 1.3 %shard_map.146 = (bf16[64,1024]{1,0:T(8,128)(2,1)}, bf16[64,1024]{1,0:T(8,128)(2,1)}, bf16[64,1024]{1,0:T(8,128)(2,1)}, bf16[64,1024]{1,0:T(8,128)(2,1)}, f32[1,64]{1,0:T(1,128)}, /*index=5*/f32[64,1024]{1,0:T(8,128)}) custom-call(f32[3,8,64,128]{3,2,1,0:T(8,128)S(1)} %get-tuple-element.19.gbuf, f32[8,8,128]{2,1,0:T(8,128)S(1)} %get-tuple-element.20.dgot, ...), custom_call_target="tpu_custom_call" | custom-call | tf_op jit(solution)/shard_map/pallas_call | solution.py:270

commit v2 on v1

v2 whole, which is shorter than its diff:
```python
import functools
import math

import jax
import jax.numpy as jnp
import numpy as np
from jax import lax
from jax.experimental import pallas as pl
from jax.experimental.pallas import tpu as pltpu
from jax.sharding import PartitionSpec as P

LANES = 128
SUB = 8
F32 = jnp.float32
BF16 = jnp.bfloat16


def halves(table):
    high = table.astype(jnp.bfloat16)
    low = (table - high.astype(np.float64)).astype(jnp.bfloat16)
    return high, low


def tables(rows, padded):
    a = np.arange(rows)[:, None]
    b = np.arange(rows)[None, :] + 0.5
    theta = 2.0 * math.pi * a * b / (2 * rows)
    first = np.concatenate([np.cos(theta).T, -np.sin(theta).T], axis=0)
    last = np.concatenate([np.cos(theta), np.sin(theta)], axis=1) * (2.0 / padded)
    r = np.arange(LANES)
    phi = 2.0 * math.pi * (np.arange(rows)[:, None] + 0.5) * r[None, :] / padded
    turn = np.stack([np.cos(phi), -np.sin(phi)]).astype(np.float32)
    psi = 2.0 * math.pi * np.outer(r, r) / LANES
    cos_m, sin_m = np.cos(psi), np.sin(psi)
    mid = np.block([[cos_m, -sin_m], [sin_m, cos_m]])
    f_hi, f_lo = halves(first)
    m_hi, m_lo = halves(mid)
    l_hi, l_lo = halves(last)
    return (
        np.concatenate([f_hi, f_hi, f_lo], axis=1),
        np.concatenate([m_hi, m_hi, m_lo], axis=0),
        np.concatenate([l_hi, l_hi, l_lo], axis=1),
        turn,
    )


def split(value, axis):
    high = value.astype(BF16)
    low = (value - high.astype(F32)).astype(BF16)
    return jnp.concatenate([high, low, high], axis=axis)


def dot(left, right):
    return jnp.dot(left, right, preferred_element_type=F32)


def fill(pairs, sems):
    copies = [pltpu.make_async_copy(src, dst, sems.at[i]) for i, (src, dst) in enumerate(pairs)]
    for copy in copies:
        copy.start()
    return copies


def exchange(
    n, chunks,
    h_post, h_pre, h_sig, h_cot, h_taps, h_first, h_mid, h_last, h_turn, h_skip,
    o_out, o_post, o_pre, o_sig, o_skip, o_taps,
    post, pre, sig, cot, taps, first, mid, last, turn, skip, sbuf, rbuf, obuf, gbuf, dsum, dgot,
    load_sem, self_sem, s_in, r_in, s_out, r_out, s_sum, r_sum,
):
    me = lax.axis_index("seq")
    chans, length = taps.shape
    blocks = length // LANES
    rows = n * blocks
    group = chans // chunks
    per = group // n
    step = per * blocks
    scale = 1.0 / math.sqrt(n * length)

    barrier = pltpu.get_barrier_semaphore()
    for k in range(1, n):
        pl.semaphore_signal(barrier, inc=1, device_id={"seq": lax.rem(me + k, n)})
    loads = fill(
        [(h_taps, taps), (h_pre, pre), (h_sig, sig), (h_cot, cot), (h_post, post),
         (h_first, first), (h_mid, mid), (h_turn, turn), (h_last, last), (h_skip, skip)], load_sem)
    for load in loads[:5]:
        load.wait()

    def peer(k):
        return lax.rem(me + k, n)

    def rows_of(t):
        return pl.ds(pl.multiple_of(t * step, step), step)

    def inward(c, k):
        return pltpu.make_async_remote_copy(
            src_ref=sbuf.at[:, c, rows_of(peer(k))], dst_ref=rbuf.at[:, c, me],
            send_sem=s_in.at[c, k], recv_sem=r_in.at[c, k], device_id={"seq": peer(k)},
        )

    def outward(c, k):
        return pltpu.make_async_remote_copy(
            src_ref=obuf.at[:, c, peer(k)], dst_ref=gbuf.at[:, c, rows_of(me)],
            send_sem=s_out.at[c, k], recv_sem=r_out.at[c, k], device_id={"seq": peer(k)},
        )

    def summed(k):
        return pltpu.make_async_remote_copy(
            src_ref=dsum, dst_ref=dgot.at[me],
            send_sem=s_sum.at[k], recv_sem=r_sum.at[k], device_id={"seq": peer(k)},
        )

    def kept_in(c):
        return pltpu.make_async_copy(sbuf.at[:, c, rows_of(me)], rbuf.at[:, c, me], self_sem.at[0, c])

    def kept_out(c):
        return pltpu.make_async_copy(obuf.at[:, c, me], gbuf.at[:, c, rows_of(me)], self_sem.at[1, c])

    for c in range(chunks):
        for q in range(blocks):
            at = (slice(group * c, group * (c + 1)), slice(LANES * q, LANES * (q + 1)))
            gated = pre[at].astype(F32) * sig[at].astype(F32)
            slope = cot[at].astype(F32) * post[at].astype(F32)
            for f, value in enumerate((taps[at], gated, slope)):
                for half in range(group // SUB):
                    sbuf[f, c, pl.ds(q + half * SUB * blocks, SUB, stride=blocks), :] = value[SUB * half:SUB * (half + 1)]
        if c == 0:
            pl.semaphore_wait(barrier, n - 1)
        for k in range(1, n):
            inward(c, k).start()
        kept_in(c).start()
    for load in loads[5:]:
        load.wait()

    def chunk(c, carry):
        for k in range(1, n):
            inward(c, k).wait()
        kept_in(c).wait()
        grown = []
        gates = []
        for f in range(3):
            xs = []
            for i in range(per):
                xs.append(rbuf[f, c, :, blocks * i:blocks * (i + 1), :].reshape(rows, LANES))
            if f == 1:
                gates = xs
            if f == 2:
                for i in range(per):
                    dsum[pl.ds(c * per + i, 1), :] = jnp.sum(gates[i] * xs[i], axis=0, keepdims=True)
            y = dot(first[...], split(jnp.concatenate(xs, axis=1), 0))
            for i in range(per):
                cut = slice(LANES * i, LANES * (i + 1))
                re, im = y[:rows, cut], y[rows:, cut]
                grown.append(jnp.concatenate([re * turn[0] - im * turn[1], re * turn[1] + im * turn[0]], axis=1))

        @pl.when(c == chunks - 1)
        def _():
            for k in range(1, n):
                summed(k).start()

        spec = dot(split(jnp.concatenate(grown, axis=0), 1), mid[...])
        prods = [[], [], []]
        for i in range(per):
            parts = []
            for f in range(3):
                top = (f * per + i) * rows
                parts.append((spec[top:top + rows, :LANES], spec[top:top + rows, LANES:]))
            (hr, hi), (gr, gi), (dr, di) = parts
            prods[0].append(jnp.concatenate([hr * gr - hi * gi, -(hr * gi + hi * gr)], axis=1))
            prods[1].append(jnp.concatenate([hr * dr + hi * di, hi * dr - hr * di], axis=1))
            prods[2].append(jnp.concatenate([gr * dr + gi * di, gi * dr - gr * di], axis=1))
        back = dot(split(jnp.concatenate(prods[0] + prods[1] + prods[2], axis=0), 1), mid[...])
        for f in range(3):
            cols = []
            for i in range(per):
                top = (f * per + i) * rows
                re, im = back[top:top + rows, :LANES], back[top:top + rows, LANES:]
                cols.append(jnp.concatenate([re * turn[0] - im * turn[1], re * turn[1] + im * turn[0]], axis=0))
            out = dot(last[...], split(jnp.concatenate(cols, axis=1), 0))
            for i in range(per):
                obuf[f, c, :, blocks * i:blocks * (i + 1), :] = out[:, LANES * i:LANES * (i + 1)].reshape(n, blocks, LANES)
        for k in range(1, n):
            outward(c, k).start()
        kept_out(c).start()
        return carry

    lax.fori_loop(0, chunks, chunk, 0)

    dgot[me] = dsum[...]
    for k in range(1, n):
        summed(k).wait()
    lane = lax.broadcasted_iota(jnp.int32, (chans, chans), 1)
    row = lax.broadcasted_iota(jnp.int32, (chans, chans), 0)
    gain = jnp.sum(jnp.where(lane == row, jnp.broadcast_to(skip[...], (chans, chans)), 0.0), axis=1, keepdims=True)
    own = chunks * per
    place = (row % own) // per * group + row // own * per + row % per
    total = jnp.sum(dgot[...].reshape(chans, LANES), axis=1, keepdims=True) * scale
    o_skip[...] = jnp.sum(jnp.where(lane == place, jnp.broadcast_to(total, (chans, chans)), 0.0), axis=0, keepdims=True)

    for c in range(chunks):
        down = slice(group * c, group * (c + 1))
        col = jnp.broadcast_to(gain[down], (group, LANES))
        for k in range(1, n):
            outward(c, k).wait()
        kept_out(c).wait()
        for q in range(blocks):
            at = (down, slice(LANES * q, LANES * (q + 1)))
            got = []
            for f in range(3):
                got.append(jnp.concatenate(
                    [gbuf[f, c, pl.ds(q + half * SUB * blocks, SUB, stride=blocks), :] for half in range(group // SUB)], axis=0))
            post_f, pre_f = post[at].astype(F32), pre[at].astype(F32)
            sig_f, cot_f = sig[at].astype(F32), cot[at].astype(F32)
            conved = got[0] + col * (pre_f * sig_f)
            o_out[at] = (post_f * conved).astype(BF16)
            o_post[at] = (cot_f * conved).astype(BF16)
            d_gated = got[1] + col * (cot_f * post_f)
            o_pre[at] = (d_gated * sig_f).astype(BF16)
            o_sig[at] = (d_gated * pre_f).astype(BF16)
            o_taps[at] = got[2] * scale


def store(*refs):
    half = len(refs) // 2
    for copy in fill(list(zip(refs[:half], refs[half:-1])), refs[-1]):
        copy.wait()


def solution(mesh):
    n = mesh.shape["seq"]
    chunks = 4

    def shards(post_gate, pre_gate, signal, cotangent, filter_taps, skip_gain):
        chans, length = filter_taps.shape
        blocks = length // LANES
        own = chans // n
        per = own // chunks
        first, mid, last, turn = tables(n * blocks, 2 * n * length)
        vmem = pl.BlockSpec(memory_space=pltpu.VMEM)
        hbm = pl.BlockSpec(memory_space=pltpu.HBM)
        half = jax.ShapeDtypeStruct((chans, length), BF16)
        results = (half, half, half, half, jax.ShapeDtypeStruct((1, chans), F32), jax.ShapeDtypeStruct((chans, length), F32))
        gates = pltpu.VMEM((chans, length), BF16)
        flat = pltpu.VMEM((3, chunks, n * per * blocks, LANES), F32)
        cut = pltpu.VMEM((3, chunks, n, per * blocks, LANES), F32)
        sem = pltpu.SemaphoreType.DMA((chunks, n))
        operands = (post_gate, pre_gate, signal, cotangent, filter_taps, first, mid, last, turn, skip_gain.reshape(1, chans))
        got = pl.pallas_call(
            functools.partial(exchange, n, chunks),
            out_shape=results,
            in_specs=[hbm] * 10,
            out_specs=[vmem] * 6,
            scratch_shapes=[
                gates, gates, gates, gates, pltpu.VMEM((chans, length), F32),
                pltpu.VMEM(first.shape, BF16), pltpu.VMEM(mid.shape, BF16), pltpu.VMEM(last.shape, BF16), pltpu.VMEM(turn.shape, F32),
                pltpu.VMEM((1, chans), F32),
                flat, cut, cut, flat,
                pltpu.VMEM((own, LANES), F32), pltpu.VMEM((n, own, LANES), F32),
                pltpu.SemaphoreType.DMA((10,)),
                pltpu.SemaphoreType.DMA((2, chunks)), sem, sem, sem, sem,
                pltpu.SemaphoreType.DMA((n,)), pltpu.SemaphoreType.DMA((n,)),
            ],
            compiler_params=pltpu.CompilerParams(collective_id=0, has_side_effects=True, vmem_limit_bytes=32 << 20),
        )(*[pltpu.with_memory_space_constraint(x, pltpu.HBM) for x in operands])
        outs = pl.pallas_call(
            store,
            out_shape=results,
            in_specs=[vmem] * 6,
            out_specs=[hbm] * 6,
            scratch_shapes=[pltpu.SemaphoreType.DMA((6,))],
            compiler_params=pltpu.CompilerParams(vmem_limit_bytes=32 << 20),
        )(*got)
        return outs[0], outs[1], outs[2], outs[3], outs[4].reshape(chans), outs[5]

    return jax.shard_map(
        shards,
        mesh=mesh,
        in_specs=(P("chan", "seq"),) * 5 + (P("chan"),),
        out_specs=(P("chan", "seq"),) * 4 + (P("chan"), P("chan", "seq")),
        check_vma=False,
    )
```

time: 26.8 us -> 26.2 us (0.978)
  Pallas kernels: 26.1 us -> 25.5 us
    pallas_call x2, Pallas kernels: 26.1 us -> 25.5 us  [the longest x1 24.5 us: shards(): pl.pallas_call(functools.partial(exchange, n, chunks), out_shape=results,...]
where the time goes in v2:
time: 26.2 us; the launch traced here: 26.1 us
  Pallas kernels  25.5 us (97%)
  between operations  0.64 us (2%)
    pallas_call x1, Pallas kernels, shards(): pl.pallas_call(functools.partial(exchange, n, chunks), out_shape=results,...  24.5 us
    pallas_call x1, Pallas kernels, shards(): pl.pallas_call(store, out_shape=results, in_specs=[vmem] * 6, out_specs=[...  0.93 us

profile of v2, /device:TPU:32, one launch (start us, length us, event | category | flops | bytes accessed | tf_op | source)
XLA Modules:
  0.0 26.1 jit_solution(12457594214212587139)
XLA Ops:
  0.6 24.5 %shard_map.145 = (bf16[64,1024]{1,0:T(8,128)(2,1)S(1)}, bf16[64,1024]{1,0:T(8,128)(2,1)S(1)}, bf16[64,1024]{1,0:T(8,128)(2,1)S(1)}, bf16[64,1024]{1,0:T(8,128)(2...) custom-call(bf16[64,1024]{1,0:T(8,128)(2,1)} %h_post.1, bf16[64,1024]{1,0:T(8,128)(2,1)} %h_pre.1, ...), custom_call_target="tpu_custom_call" | custom-call | tf_op jit(solution)/shard_map/pallas_call | solution.py:248
  25.2 0.9 %shard_map.146 = (bf16[64,1024]{1,0:T(8,128)(2,1)}, bf16[64,1024]{1,0:T(8,128)(2,1)}, bf16[64,1024]{1,0:T(8,128)(2,1)}, bf16[64,1024]{1,0:T(8,128)(2,1)}, f32[1,64]{1,0:T(1,128)}, /*index=5*/f32[64,1024]{1,0:T(8,128)}) custom-call(bf16[64,1024]{1,0:T(8,128)(2,1)S(1)} %get-tuple-element.18.refs_0_, bf16[64,1024]{1,0:T(8,128)(2,1)S(1)} %get-tuple-element.19.refs_1_, ...), custom_call_target="tpu_custom_call" | custom-call | tf_op jit(solution)/shard_map/pallas_call | solution.py:265

commit v3 on v2

--- a/solution.py
+++ b/solution.py
@@ -62,10 +62,10 @@
 
 
 def exchange(
-    n, chunks,
+    n, chunks, join,
     h_post, h_pre, h_sig, h_cot, h_taps, h_first, h_mid, h_last, h_turn, h_skip,
     o_out, o_post, o_pre, o_sig, o_skip, o_taps,
-    post, pre, sig, cot, taps, first, mid, last, turn, skip, sbuf, rbuf, obuf, gbuf, dsum, dgot,
+    post, pre, sig, cot, taps, first, mid, last, turn, skip, sbuf, rbuf, obuf, gbuf, dsum, dgot, sums,
     load_sem, self_sem, s_in, r_in, s_out, r_out, s_sum, r_sum,
 ):
     me = lax.axis_index("seq")
@@ -75,6 +75,7 @@
     group = chans // chunks
     per = group // n
     step = per * blocks
+    tall = 3 * step
     scale = 1.0 / math.sqrt(n * length)
 
     barrier = pltpu.get_barrier_semaphore()
@@ -89,18 +90,24 @@
     def peer(k):
         return lax.rem(me + k, n)
 
+    def wide_of(t):
+        return pl.ds(pl.multiple_of(t * join * tall, join * tall), join * tall)
+
     def rows_of(t):
-        return pl.ds(pl.multiple_of(t * step, step), step)
+        return pl.ds(pl.multiple_of(t * tall, tall), tall)
+
+    def spread(f, i, q, more=0, wide=1):
+        return pl.ds(more * tall + f * step + i * blocks + q, n, stride=wide * tall)
 
     def inward(c, k):
         return pltpu.make_async_remote_copy(
-            src_ref=sbuf.at[:, c, rows_of(peer(k))], dst_ref=rbuf.at[:, c, me],
+            src_ref=sbuf.at[c, rows_of(peer(k))], dst_ref=rbuf.at[c, me],
             send_sem=s_in.at[c, k], recv_sem=r_in.at[c, k], device_id={"seq": peer(k)},
         )
 
     def outward(c, k):
         return pltpu.make_async_remote_copy(
-            src_ref=obuf.at[:, c, peer(k)], dst_ref=gbuf.at[:, c, rows_of(me)],
+            src_ref=obuf.at[c, peer(k)], dst_ref=gbuf.at[c, wide_of(me)],
             send_sem=s_out.at[c, k], recv_sem=r_out.at[c, k], device_id={"seq": peer(k)},
         )
 
@@ -111,10 +118,10 @@
         )
 
     def kept_in(c):
-        return pltpu.make_async_copy(sbuf.at[:, c, rows_of(me)], rbuf.at[:, c, me], self_sem.at[0, c])
+        return pltpu.make_async_copy(sbuf.at[c, rows_of(me)], rbuf.at[c, me], self_sem.at[0, c])
 
     def kept_out(c):
-        return pltpu.make_async_copy(obuf.at[:, c, me], gbuf.at[:, c, rows_of(me)], self_sem.at[1, c])
+        return pltpu.make_async_copy(obuf.at[c, me], gbuf.at[c, wide_of(me)], self_sem.at[1, c])
 
     for c in range(chunks):
         for q in range(blocks):
@@ -122,8 +129,8 @@
             gated = pre[at].astype(F32) * sig[at].astype(F32)
             slope = cot[at].astype(F32) * post[at].astype(F32)
             for f, value in enumerate((taps[at], gated, slope)):
-                for half in range(group // SUB):
-                    sbuf[f, c, pl.ds(q + half * SUB * blocks, SUB, stride=blocks), :] = value[SUB * half:SUB * (half + 1)]
+                for i in range(per):
+                    sbuf[c, spread(f, i, q), :] = value[n * i:n * (i + 1)]
         if c == 0:
             pl.semaphore_wait(barrier, n - 1)
         for k in range(1, n):
@@ -131,6 +138,9 @@
         kept_in(c).start()
     for load in loads[5:]:
         load.wait()
+
+    spot = lax.broadcasted_iota(jnp.int32, (1, LANES), 1)
+    dsum[...] = jnp.zeros_like(dsum)
 
     def chunk(c, carry):
         for k in range(1, n):
@@ -141,12 +151,14 @@
         for f in range(3):
             xs = []
             for i in range(per):
-                xs.append(rbuf[f, c, :, blocks * i:blocks * (i + 1), :].reshape(rows, LANES))
+                top = f * step + i * blocks
+                xs.append(rbuf[c, :, top:top + blocks, :].reshape(rows, LANES))
             if f == 1:
                 gates = xs
             if f == 2:
                 for i in range(per):
-                    dsum[pl.ds(c * per + i, 1), :] = jnp.sum(gates[i] * xs[i], axis=0, keepdims=True)
+                    total = jnp.sum(jnp.sum(gates[i] * xs[i], axis=0, keepdims=True), axis=1, keepdims=True)
+                    dsum[...] = jnp.where(spot == c * per + i, total, dsum[...])
             y = dot(first[...], split(jnp.concatenate(xs, axis=1), 0))
             for i in range(per):
                 cut = slice(LANES * i, LANES * (i + 1))
@@ -178,10 +190,15 @@
                 cols.append(jnp.concatenate([re * turn[0] - im * turn[1], re * turn[1] + im * turn[0]], axis=0))
             out = dot(last[...], split(jnp.concatenate(cols, axis=1), 0))
             for i in range(per):
-                obuf[f, c, :, blocks * i:blocks * (i + 1), :] = out[:, LANES * i:LANES * (i + 1)].reshape(n, blocks, LANES)
-        for k in range(1, n):
-            outward(c, k).start()
-        kept_out(c).start()
+                top = pl.multiple_of(lax.rem(c, join) * tall + f * step + i * blocks, blocks)
+                obuf[c // join, :, pl.ds(top, blocks), :] = out[:, LANES * i:LANES * (i + 1)].reshape(n, blocks, LANES)
+
+        @pl.when(lax.rem(c, join) == join - 1)
+        def _():
+            for k in range(1, n):
+                outward(c // join, k).start()
+            kept_out(c // join).start()
+
         return carry
 
     lax.fori_loop(0, chunks, chunk, 0)
@@ -192,23 +209,28 @@
     lane = lax.broadcasted_iota(jnp.int32, (chans, chans), 1)
     row = lax.broadcasted_iota(jnp.int32, (chans, chans), 0)
     gain = jnp.sum(jnp.where(lane == row, jnp.broadcast_to(skip[...], (chans, chans)), 0.0), axis=1, keepdims=True)
-    own = chunks * per
-    place = (row % own) // per * group + row // own * per + row % per
-    total = jnp.sum(dgot[...].reshape(chans, LANES), axis=1, keepdims=True) * scale
-    o_skip[...] = jnp.sum(jnp.where(lane == place, jnp.broadcast_to(total, (chans, chans)), 0.0), axis=0, keepdims=True)
+    for t in range(n):
+        sums[t:t + 1, :] = dgot[t]
+    found = sums[...]
+    lane = lax.broadcasted_iota(jnp.int32, (n, chans), 1)
+    row = lax.broadcasted_iota(jnp.int32, (n, chans), 0)
+    line = jnp.zeros((n, chans), F32)
+    for j in range(chunks * per):
+        line = jnp.where(lane == j * n + row, found[:, j:j + 1], line)
+    o_skip[...] = jnp.sum(line, axis=0, keepdims=True) * scale
 
     for c in range(chunks):
         down = slice(group * c, group * (c + 1))
         col = jnp.broadcast_to(gain[down], (group, LANES))
-        for k in range(1, n):
-            outward(c, k).wait()
-        kept_out(c).wait()
+        if c % join == 0:
+            for k in range(1, n):
+                outward(c // join, k).wait()
+            kept_out(c // join).wait()
         for q in range(blocks):
             at = (down, slice(LANES * q, LANES * (q + 1)))
             got = []
             for f in range(3):
-                got.append(jnp.concatenate(
-                    [gbuf[f, c, pl.ds(q + half * SUB * blocks, SUB, stride=blocks), :] for half in range(group // SUB)], axis=0))
+                got.append(jnp.concatenate([gbuf[c // join, spread(f, i, q, c % join, join), :] for i in range(per)], axis=0))
             post_f, pre_f = post[at].astype(F32), pre[at].astype(F32)
             sig_f, cot_f = sig[at].astype(F32), cot[at].astype(F32)
             conved = got[0] + col * (pre_f * sig_f)
@@ -229,6 +251,7 @@
 def solution(mesh):
     n = mesh.shape["seq"]
     chunks = 4
+    join = 1
 
     def shards(post_gate, pre_gate, signal, cotangent, filter_taps, skip_gain):
         chans, length = filter_taps.shape
@@ -241,12 +264,15 @@
         half = jax.ShapeDtypeStruct((chans, length), BF16)
         results = (half, half, half, half, jax.ShapeDtypeStruct((1, chans), F32), jax.ShapeDtypeStruct((chans, length), F32))
         gates = pltpu.VMEM((chans, length), BF16)
-        flat = pltpu.VMEM((3, chunks, n * per * blocks, LANES), F32)
-        cut = pltpu.VMEM((3, chunks, n, per * blocks, LANES), F32)
+        wide = pltpu.VMEM((chunks // join, n * 3 * per * blocks * join, LANES), F32)
+        both = pltpu.VMEM((chunks // join, n, 3 * per * blocks * join, LANES), F32)
+        few = pltpu.SemaphoreType.DMA((chunks // join, n))
+        flat = pltpu.VMEM((chunks, n * 3 * per * blocks, LANES), F32)
+        cut = pltpu.VMEM((chunks, n, 3 * per * blocks, LANES), F32)
         sem = pltpu.SemaphoreType.DMA((chunks, n))
         operands = (post_gate, pre_gate, signal, cotangent, filter_taps, first, mid, last, turn, skip_gain.reshape(1, chans))
         got = pl.pallas_call(
-            functools.partial(exchange, n, chunks),
+            functools.partial(exchange, n, chunks, join),
             out_shape=results,
             in_specs=[hbm] * 10,
             out_specs=[vmem] * 6,
@@ -254,10 +280,10 @@
                 gates, gates, gates, gates, pltpu.VMEM((chans, length), F32),
                 pltpu.VMEM(first.shape, BF16), pltpu.VMEM(mid.shape, BF16), pltpu.VMEM(last.shape, BF16), pltpu.VMEM(turn.shape, F32),
                 pltpu.VMEM((1, chans), F32),
-                flat, cut, cut, flat,
-                pltpu.VMEM((own, LANES), F32), pltpu.VMEM((n, own, LANES), F32),
+                flat, cut, both, wide,
+                pltpu.VMEM((1, LANES), F32), pltpu.VMEM((n, 1, LANES), F32), pltpu.VMEM((n, LANES), F32),
                 pltpu.SemaphoreType.DMA((10,)),
-                pltpu.SemaphoreType.DMA((2, chunks)), sem, sem, sem, sem,
+                pltpu.SemaphoreType.DMA((2, chunks)), sem, sem, few, few,
                 pltpu.SemaphoreType.DMA((n,)), pltpu.SemaphoreType.DMA((n,)),
             ],
             compiler_params=pltpu.CompilerParams(collective_id=0, has_side_effects=True, vmem_limit_bytes=32 << 20),

time: 26.2 us -> 25.9 us (0.989)
  Pallas kernels: 25.5 us -> 25.2 us
    pallas_call x1, Pallas kernels: 24.5 us -> 24.2 us  [shards(): pl.pallas_call(functools.partial(exchange, n, chunks, join), out_shape=re...]
where the time goes in v3:
time: 25.9 us; the launch traced here: 25.8 us
  Pallas kernels  25.2 us (97%)
  between operations  0.64 us (2%)
    pallas_call x1, Pallas kernels, shards(): pl.pallas_call(functools.partial(exchange, n, chunks, join), out_shape=re...  24.2 us
    pallas_call x1, Pallas kernels, shards(): pl.pallas_call(store, out_shape=results, in_specs=[vmem] * 6, out_specs=[...  0.93 us

profile of v3, /device:TPU:32, one launch (start us, length us, event | category | flops | bytes accessed | tf_op | source)
XLA Modules:
  0.0 25.8 jit_solution(16387521481642715511)
XLA Ops:
  0.6 24.2 %shard_map.145 = (bf16[64,1024]{1,0:T(8,128)(2,1)S(1)}, bf16[64,1024]{1,0:T(8,128)(2,1)S(1)}, bf16[64,1024]{1,0:T(8,128)(2,1)S(1)}, bf16[64,1024]{1,0:T(8,128)(2...) custom-call(bf16[64,1024]{1,0:T(8,128)(2,1)} %h_post.1, bf16[64,1024]{1,0:T(8,128)(2,1)} %h_pre.1, ...), custom_call_target="tpu_custom_call" | custom-call | tf_op jit(solution)/shard_map/pallas_call | solution.py:274
  24.9 0.9 %shard_map.146 = (bf16[64,1024]{1,0:T(8,128)(2,1)}, bf16[64,1024]{1,0:T(8,128)(2,1)}, bf16[64,1024]{1,0:T(8,128)(2,1)}, bf16[64,1024]{1,0:T(8,128)(2,1)}, f32[1,64]{1,0:T(1,128)}, /*index=5*/f32[64,1024]{1,0:T(8,128)}) custom-call(bf16[64,1024]{1,0:T(8,128)(2,1)S(1)} %get-tuple-element.18.refs_0_, bf16[64,1024]{1,0:T(8,128)(2,1)S(1)} %get-tuple-element.19.refs_1_, ...), custom_call_target="tpu_custom_call" | custom-call | tf_op jit(solution)/shard_map/pallas_call | solution.py:291

commit v4 on v3

--- a/solution.py
+++ b/solution.py
@@ -61,11 +61,33 @@
     return copies
 
 
+def weigh(c, n, per, down, to, col, gbuf, post, pre, sig, cot, o_out, o_post, o_pre, o_sig, o_taps):
+    blocks = post.shape[1] // LANES
+    step = per * blocks
+    scale = 1.0 / math.sqrt(n * post.shape[1])
+    for q in range(blocks):
+        side = slice(LANES * q, LANES * (q + 1))
+        at, put = (down, side), (to, side)
+        got = []
+        for f in range(3):
+            got.append(jnp.concatenate(
+                [gbuf[c, pl.ds(f * step + i * blocks + q, n, stride=3 * step), :] for i in range(per)], axis=0))
+        post_f, pre_f = post[at].astype(F32), pre[at].astype(F32)
+        sig_f, cot_f = sig[at].astype(F32), cot[at].astype(F32)
+        conved = got[0] + col * (pre_f * sig_f)
+        o_out[put] = (post_f * conved).astype(BF16)
+        o_post[put] = (cot_f * conved).astype(BF16)
+        d_gated = got[1] + col * (cot_f * post_f)
+        o_pre[put] = (d_gated * sig_f).astype(BF16)
+        o_sig[put] = (d_gated * pre_f).astype(BF16)
+        o_taps[put] = got[2] * scale
+
+
 def exchange(
     n, chunks, join,
     h_post, h_pre, h_sig, h_cot, h_taps, h_first, h_mid, h_last, h_turn, h_skip,
-    o_out, o_post, o_pre, o_sig, o_skip, o_taps,
-    post, pre, sig, cot, taps, first, mid, last, turn, skip, sbuf, rbuf, obuf, gbuf, dsum, dgot, sums,
+    o_out, o_post, o_pre, o_sig, o_skip, o_taps, gbuf, post, pre, sig, cot, wide_gain,
+    taps, first, mid, last, turn, skip, sbuf, rbuf, obuf, dsum, dgot, sums,
     load_sem, self_sem, s_in, r_in, s_out, r_out, s_sum, r_sum,
 ):
     me = lax.axis_index("seq")
@@ -226,25 +248,23 @@
             for k in range(1, n):
                 outward(c // join, k).wait()
             kept_out(c // join).wait()
-        for q in range(blocks):
-            at = (down, slice(LANES * q, LANES * (q + 1)))
-            got = []
-            for f in range(3):
-                got.append(jnp.concatenate([gbuf[c // join, spread(f, i, q, c % join, join), :] for i in range(per)], axis=0))
-            post_f, pre_f = post[at].astype(F32), pre[at].astype(F32)
-            sig_f, cot_f = sig[at].astype(F32), cot[at].astype(F32)
-            conved = got[0] + col * (pre_f * sig_f)
-            o_out[at] = (post_f * conved).astype(BF16)
-            o_post[at] = (cot_f * conved).astype(BF16)
-            d_gated = got[1] + col * (cot_f * post_f)
-            o_pre[at] = (d_gated * sig_f).astype(BF16)
-            o_sig[at] = (d_gated * pre_f).astype(BF16)
-            o_taps[at] = got[2] * scale
-
-
-def store(*refs):
-    half = len(refs) // 2
-    for copy in fill(list(zip(refs[:half], refs[half:-1])), refs[-1]):
+        if c < chunks - 1:
+            weigh(c, n, per, down, down, col, gbuf, post, pre, sig, cot, o_out, o_post, o_pre, o_sig, o_taps)
+    wide_gain[...] = jnp.broadcast_to(gain[group * (chunks - 1):], wide_gain.shape)
+
+
+def store(n, per, r_out, r_post, r_pre, r_sig, r_skip, r_taps, gbuf, post, pre, sig, cot, wide_gain,
+          h_out, h_post, h_pre, h_sig, h_skip, h_taps, l_out, l_post, l_pre, l_sig, l_taps, sems):
+    chans = post.shape[0]
+    group = n * per
+    head, tail = slice(0, chans - group), slice(chans - group, chans)
+    ends = (h_out, h_post, h_pre, h_sig, h_taps)
+    copies = fill([(src.at[head], dst.at[head]) for src, dst in zip((r_out, r_post, r_pre, r_sig, r_taps), ends)]
+                  + [(r_skip, h_skip)], sems.at[0])
+    rest = (l_out, l_post, l_pre, l_sig, l_taps)
+    weigh(gbuf.shape[0] - 1, n, per, tail, slice(0, group), wide_gain[...], gbuf, post, pre, sig, cot, *rest)
+    copies += fill([(src, dst.at[tail]) for src, dst in zip(rest, ends)], sems.at[1])
+    for copy in copies:
         copy.wait()
 
 
@@ -263,8 +283,8 @@
         hbm = pl.BlockSpec(memory_space=pltpu.HBM)
         half = jax.ShapeDtypeStruct((chans, length), BF16)
         results = (half, half, half, half, jax.ShapeDtypeStruct((1, chans), F32), jax.ShapeDtypeStruct((chans, length), F32))
-        gates = pltpu.VMEM((chans, length), BF16)
-        wide = pltpu.VMEM((chunks // join, n * 3 * per * blocks * join, LANES), F32)
+        carried = (jax.ShapeDtypeStruct((chunks // join, n * 3 * per * blocks * join, LANES), F32),
+                   half, half, half, half, jax.ShapeDtypeStruct((n * per, LANES), F32))
         both = pltpu.VMEM((chunks // join, n, 3 * per * blocks * join, LANES), F32)
         few = pltpu.SemaphoreType.DMA((chunks // join, n))
         flat = pltpu.VMEM((chunks, n * 3 * per * blocks, LANES), F32)
@@ -273,14 +293,14 @@
         operands = (post_gate, pre_gate, signal, cotangent, filter_taps, first, mid, last, turn, skip_gain.reshape(1, chans))
         got = pl.pallas_call(
             functools.partial(exchange, n, chunks, join),
-            out_shape=results,
+            out_shape=results + carried,
             in_specs=[hbm] * 10,
-            out_specs=[vmem] * 6,
+            out_specs=[vmem] * 12,
             scratch_shapes=[
-                gates, gates, gates, gates, pltpu.VMEM((chans, length), F32),
+                pltpu.VMEM((chans, length), F32),
                 pltpu.VMEM(first.shape, BF16), pltpu.VMEM(mid.shape, BF16), pltpu.VMEM(last.shape, BF16), pltpu.VMEM(turn.shape, F32),
                 pltpu.VMEM((1, chans), F32),
-                flat, cut, both, wide,
+                flat, cut, both,
                 pltpu.VMEM((1, LANES), F32), pltpu.VMEM((n, 1, LANES), F32), pltpu.VMEM((n, LANES), F32),
                 pltpu.SemaphoreType.DMA((10,)),
                 pltpu.SemaphoreType.DMA((2, chunks)), sem, sem, few, few,
@@ -289,11 +309,12 @@
             compiler_params=pltpu.CompilerParams(collective_id=0, has_side_effects=True, vmem_limit_bytes=32 << 20),
         )(*[pltpu.with_memory_space_constraint(x, pltpu.HBM) for x in operands])
         outs = pl.pallas_call(
-            store,
+            functools.partial(store, n, per),
             out_shape=results,
-            in_specs=[vmem] * 6,
+            in_specs=[vmem] * 12,
             out_specs=[hbm] * 6,
-            scratch_shapes=[pltpu.SemaphoreType.DMA((6,))],
+            scratch_shapes=[pltpu.VMEM((n * per, length), BF16)] * 4 + [
+                pltpu.VMEM((n * per, length), F32), pltpu.SemaphoreType.DMA((2, 6))],
             compiler_params=pltpu.CompilerParams(vmem_limit_bytes=32 << 20),
         )(*got)
         return outs[0], outs[1], outs[2], outs[3], outs[4].reshape(chans), outs[5]

time: 25.9 us -> 25.9 us (level)
  no operation moved by 1% of the time
where the time goes in v4:
time: 25.9 us; the launch traced here: 25.8 us
  Pallas kernels  25.2 us (97%)
  between operations  0.64 us (2%)
    pallas_call x1, Pallas kernels, shards(): pl.pallas_call(functools.partial(exchange, n, chunks, join), out_shape=re...  24.2 us
    pallas_call x1, Pallas kernels, shards(): pl.pallas_call(functools.partial(store, n, per), out_shape=results, in_sp...  0.98 us

profile of v4, /device:TPU:32, one launch (start us, length us, event | category | flops | bytes accessed | tf_op | source)
XLA Modules:
  0.0 25.8 jit_solution(16915436606184768796)
XLA Ops:
  0.6 24.2 %shard_map.145 = (bf16[64,1024]{1,0:T(8,128)(2,1)S(1)}, bf16[64,1024]{1,0:T(8,128)(2,1)S(1)}, bf16[64,1024]{1,0:T(8,128)(2,1)S(1)}, bf16[64,1024]{1,0:T(8,128)(2...) custom-call(bf16[64,1024]{1,0:T(8,128)(2,1)} %h_post.1, ...), custom_call_target="tpu_custom_call" | custom-call | tf_op jit(solution)/shard_map/pallas_call | solution.py:294
  24.8 1.0 %shard_map.146 = (bf16[64,1024]{1,0:T(8,128)(2,1)}, bf16[64,1024]{1,0:T(8,128)(2,1)}, bf16[64,1024]{1,0:T(8,128)(2,1)}, bf16[64,1024]{1,0:T(8,128)(2,1)}, f32[1,64]{1,0:T(1,128)}, /*index=5*/f32[64,1024]{1,0:T(8,128)}) custom-call(bf16[64,1024]{1,0:T(8,128)(2,1)S(1)} %get-tuple-element.24.r_out, bf16[64,1024]{1,0:T(8,128)(2,1)S(1)} %get-tuple-element.25.r_post, ...), custom_call_target="tpu_custom_call" | custom-call | tf_op jit(solution)/shard_map/pallas_call | solution.py:311

commit v5 on v3

--- a/solution.py
+++ b/solution.py
@@ -65,7 +65,7 @@
     n, chunks, join,
     h_post, h_pre, h_sig, h_cot, h_taps, h_first, h_mid, h_last, h_turn, h_skip,
     o_out, o_post, o_pre, o_sig, o_skip, o_taps,
-    post, pre, sig, cot, taps, first, mid, last, turn, skip, sbuf, rbuf, obuf, gbuf, dsum, dgot, sums,
+    post, pre, sig, cot, taps, first, mid, last, turn, skip, sbuf, rbuf, obuf, gbuf, dsum, dgot, sums, gains,
     load_sem, self_sem, s_in, r_in, s_out, r_out, s_sum, r_sum,
 ):
     me = lax.axis_index("seq")
@@ -219,18 +219,19 @@
         line = jnp.where(lane == j * n + row, found[:, j:j + 1], line)
     o_skip[...] = jnp.sum(line, axis=0, keepdims=True) * scale
 
-    for c in range(chunks):
-        down = slice(group * c, group * (c + 1))
-        col = jnp.broadcast_to(gain[down], (group, LANES))
-        if c % join == 0:
-            for k in range(1, n):
-                outward(c // join, k).wait()
-            kept_out(c // join).wait()
+    gains[...] = jnp.broadcast_to(gain, gains.shape)
+
+    def settle(c, carry):
+        down = pl.ds(pl.multiple_of(c * group, group), group)
+        col = gains[down, :]
+        for k in range(1, n):
+            outward(c, k).wait()
+        kept_out(c).wait()
         for q in range(blocks):
             at = (down, slice(LANES * q, LANES * (q + 1)))
             got = []
             for f in range(3):
-                got.append(jnp.concatenate([gbuf[c // join, spread(f, i, q, c % join, join), :] for i in range(per)], axis=0))
+                got.append(jnp.concatenate([gbuf[c, spread(f, i, q), :] for i in range(per)], axis=0))
             post_f, pre_f = post[at].astype(F32), pre[at].astype(F32)
             sig_f, cot_f = sig[at].astype(F32), cot[at].astype(F32)
             conved = got[0] + col * (pre_f * sig_f)
@@ -240,6 +241,9 @@
             o_pre[at] = (d_gated * sig_f).astype(BF16)
             o_sig[at] = (d_gated * pre_f).astype(BF16)
             o_taps[at] = got[2] * scale
+        return carry
+
+    lax.fori_loop(0, chunks, settle, 0)
 
 
 def store(*refs):
@@ -282,6 +286,7 @@
                 pltpu.VMEM((1, chans), F32),
                 flat, cut, both, wide,
                 pltpu.VMEM((1, LANES), F32), pltpu.VMEM((n, 1, LANES), F32), pltpu.VMEM((n, LANES), F32),
+                pltpu.VMEM((chans, LANES), F32),
                 pltpu.SemaphoreType.DMA((10,)),
                 pltpu.SemaphoreType.DMA((2, chunks)), sem, sem, few, few,
                 pltpu.SemaphoreType.DMA((n,)), pltpu.SemaphoreType.DMA((n,)),

time: 25.9 us -> 25.9 us (level)
  no operation moved by 1% of the time
where the time goes in v5:
time: 25.9 us; the launch traced here: 25.8 us
  Pallas kernels  25.2 us (97%)
  between operations  0.64 us (2%)
    pallas_call x1, Pallas kernels, shards(): pl.pallas_call(functools.partial(exchange, n, chunks, join), out_shape=re...  24.2 us
    pallas_call x1, Pallas kernels, shards(): pl.pallas_call(store, out_shape=results, in_specs=[vmem] * 6, out_specs=[...  0.93 us

profile of v5, /device:TPU:32, one launch (start us, length us, event | category | flops | bytes accessed | tf_op | source)
XLA Modules:
  0.0 25.8 jit_solution(4623768238056040412)
XLA Ops:
  0.6 24.2 %shard_map.145 = (bf16[64,1024]{1,0:T(8,128)(2,1)S(1)}, bf16[64,1024]{1,0:T(8,128)(2,1)S(1)}, bf16[64,1024]{1,0:T(8,128)(2,1)S(1)}, bf16[64,1024]{1,0:T(8,128)(2...) custom-call(bf16[64,1024]{1,0:T(8,128)(2,1)} %h_post.1, bf16[64,1024]{1,0:T(8,128)(2,1)} %h_pre.1, ...), custom_call_target="tpu_custom_call" | custom-call | tf_op jit(solution)/shard_map/pallas_call | solution.py:278
  24.9 0.9 %shard_map.146 = (bf16[64,1024]{1,0:T(8,128)(2,1)}, bf16[64,1024]{1,0:T(8,128)(2,1)}, bf16[64,1024]{1,0:T(8,128)(2,1)}, bf16[64,1024]{1,0:T(8,128)(2,1)}, f32[1,64]{1,0:T(1,128)}, /*index=5*/f32[64,1024]{1,0:T(8,128)}) custom-call(bf16[64,1024]{1,0:T(8,128)(2,1)S(1)} %get-tuple-element.18.refs_0_, bf16[64,1024]{1,0:T(8,128)(2,1)S(1)} %get-tuple-element.19.refs_1_, ...), custom_call_target="tpu_custom_call" | custom-call | tf_op jit(solution)/shard_map/pallas_call | solution.py:296

commit v6 on v3

--- a/solution.py
+++ b/solution.py
@@ -195,7 +195,7 @@
 
         @pl.when(lax.rem(c, join) == join - 1)
         def _():
-            for k in range(1, n):
+            for k in (2, 6, 3, 5, 1, 7, 4):
                 outward(c // join, k).start()
             kept_out(c // join).start()
 

time: 25.9 us -> 26.1 us (level)
  no operation moved by 1% of the time
where the time goes in v6:
time: 26.1 us; the launch traced here: 26 us
  Pallas kernels  25.4 us (97%)
  between operations  0.64 us (2%)
    pallas_call x1, Pallas kernels, shards(): pl.pallas_call(functools.partial(exchange, n, chunks, join), out_shape=re...  24.5 us
    pallas_call x1, Pallas kernels, shards(): pl.pallas_call(store, out_shape=results, in_specs=[vmem] * 6, out_specs=[...  0.93 us

profile of v6, /device:TPU:32, one launch (start us, length us, event | category | flops | bytes accessed | tf_op | source)
XLA Modules:
  0.0 26.0 jit_solution(16182169891643325838)
XLA Ops:
  0.6 24.5 %shard_map.145 = (bf16[64,1024]{1,0:T(8,128)(2,1)S(1)}, bf16[64,1024]{1,0:T(8,128)(2,1)S(1)}, bf16[64,1024]{1,0:T(8,128)(2,1)S(1)}, bf16[64,1024]{1,0:T(8,128)(2...) custom-call(bf16[64,1024]{1,0:T(8,128)(2,1)} %h_post.1, bf16[64,1024]{1,0:T(8,128)(2,1)} %h_pre.1, ...), custom_call_target="tpu_custom_call" | custom-call | tf_op jit(solution)/shard_map/pallas_call | solution.py:274
  25.1 0.9 %shard_map.146 = (bf16[64,1024]{1,0:T(8,128)(2,1)}, bf16[64,1024]{1,0:T(8,128)(2,1)}, bf16[64,1024]{1,0:T(8,128)(2,1)}, bf16[64,1024]{1,0:T(8,128)(2,1)}, f32[1,64]{1,0:T(1,128)}, /*index=5*/f32[64,1024]{1,0:T(8,128)}) custom-call(bf16[64,1024]{1,0:T(8,128)(2,1)S(1)} %get-tuple-element.18.refs_0_, bf16[64,1024]{1,0:T(8,128)(2,1)S(1)} %get-tuple-element.19.refs_1_, ...), custom_call_target="tpu_custom_call" | custom-call | tf_op jit(solution)/shard_map/pallas_call | solution.py:291
